TPU v7x, 32 devices: a whole 2x2x4 slice. The times are simulated.
32 devices in a mesh: ens: 8 (over z, x), mesh: 4 (over y, core).
Axes of the slice: x: 2, y: 2, z: 4, core: 2. Of those that a mesh axis runs over, the one named last changes fastest.
Arguments:
- inputs: bfloat16 [8, 1024, 512], P('ens', 'mesh'), may hold values from -6 to 6
- cotangent: bfloat16 [8, 1024, 512], P('ens', 'mesh'), may hold values from -6 to 6
- noise_level: float32 [8], P('ens'), may hold values from 0.02 to 80
- neighbours: int32 [1024, 32], P('mesh'), may hold values from 0 to 1023, as said below
- live_slots: int32 [1024, 32], P('mesh'), may hold values from 0 to 1
- projections: bfloat16 [2, 4, 512, 512], replicated, may hold values from -4 to 4
- film_weights: float32 [2, 32, 1024], replicated, may hold values from -0.5 to 0.5
Outputs:
- grad_input: bfloat16 [8, 1024, 512], P('ens', 'mesh')
- grad_projections: float32 [2, 4, 512, 512], P(None, None, 'ens', 'mesh')
- grad_film: float32 [2, 32, 1024], P(None, None, 'mesh')
Inputs may be any that keep to these rules, and one draw needn't show every extreme that they name: `neighbours`: slot 0 of node i names i and is live. The live slots of a node name distinct nodes within 128 of it; every node at least 128 from both ends of the numbering has a live slot exactly 128 away. Padded slots name the node itself.
All inputs are finite; a program needn't handle non-finite values.
Results may differ from a plain program's by a relative error of at most 0.028.
Values may be sent and summed in bfloat16 or wider, within the bound.
No kernel may reach another device: no remote copies, remote signals or barrier semaphores. Data moves between devices by JAX's collectives and lax.ppermute only.
A program may use at most 64 MiB of HBM per device.

v0:
```python
import math
import jax
import jax.numpy as jnp
from jax import lax
from jax.sharding import PartitionSpec as P

HEADS = 4
NOISE_FREQ = 16
LAYERS = 2
epsilon = 1e-05


def padded(cells, sides, width):
    for axis, dim in sides:
        count = lax.axis_size(axis)
        ends = count - 1
        head = lax.slice_in_dim(cells, 0, width, axis=dim)
        tail = lax.slice_in_dim(cells, cells.shape[dim] - width, cells.shape[dim], axis=dim)
        cells = jnp.concatenate(
            [
                lax.ppermute(tail, axis, [(i, (i + 1) % count) for i in range(ends)]),
                cells,
                lax.ppermute(head, axis, [((i + 1) % count, i) for i in range(ends)]),
            ],
            axis=dim,
        )
    return cells


def from_behind(block, axis, distance):
    devices = range(lax.axis_size(axis))
    route = [(i - distance, i) for i in devices if i - distance in devices]
    return lax.ppermute(block, axis, route)


def noise_features(noise_level):
    frequency = jnp.arange(1, NOISE_FREQ + 1).astype(jnp.float32)
    angles = jnp.log(noise_level)[:, None] * frequency[None, :]
    return jnp.concatenate([jnp.sin(angles), jnp.cos(angles)], axis=1)


def project(left_side, right_side):
    return jnp.dot(left_side, right_side, preferred_element_type=jnp.float32)


def contract_rows(left_side, right_side):
    return lax.dot_general(
        left_side, right_side, (((0,), (0,)), ((), ())), preferred_element_type=jnp.float32
    )


def contract_cols(left_side, right_side):
    return lax.dot_general(
        left_side, right_side, (((1,), (1,)), ((), ())), preferred_element_type=jnp.float32
    )


def normalize(states, film_row, model_width):
    values = states.astype(jnp.float32)
    centre = jnp.mean(values, axis=1, keepdims=True)
    spread = jnp.mean(jnp.square(values - centre), axis=1, keepdims=True)
    inverse = lax.rsqrt(spread + epsilon)
    unit_rows = (values - centre) * inverse
    normed = (unit_rows * (1.0 + film_row[:model_width]) + film_row[model_width:]).astype(
        jnp.bfloat16
    )
    return (unit_rows, inverse, normed)


def dense_attention(query_head, key_head, present, head_size):
    scores = contract_cols(query_head, key_head) / math.sqrt(head_size)
    scores = jnp.where(present, scores, -jnp.inf)
    row_peak = jnp.max(scores, axis=1, keepdims=True)
    weights = jnp.where(present, jnp.exp(scores - row_peak), 0.0)
    return weights / jnp.sum(weights, axis=1, keepdims=True)


def extend_rims(normed, weights, rim_width, model_width):
    joined = jnp.concatenate(
        [
            project(normed, weights[1]).astype(jnp.bfloat16),
            project(normed, weights[2]).astype(jnp.bfloat16),
        ],
        axis=1,
    )
    joined_ext = padded(joined, (("mesh", 0),), rim_width)
    key_ext = joined_ext[:, :model_width]
    value_ext = joined_ext[:, model_width:]
    return (key_ext, value_ext)


def body(inputs, cotangent, noise_level, neighbours, live_slots, projections, film_weights):
    current = inputs[0]
    node_count, model_width = current.shape
    head_size = model_width // HEADS
    rim_width = node_count // 2
    window = node_count + 2 * rim_width
    offset = lax.axis_index("mesh") * node_count - rim_width
    columns = neighbours - offset
    row_ids = jnp.broadcast_to(jnp.arange(node_count, dtype=jnp.int32)[:, None], columns.shape)
    adjacency = (
        jnp.zeros((node_count, window), jnp.float32)
        .at[row_ids, columns]
        .add(live_slots.astype(jnp.float32))
    )
    present = adjacency > 0.5
    embedding = noise_features(noise_level)[0]
    film_rows = [
        jnp.dot(embedding[None, :], film_weights[layer_number], precision=lax.Precision.HIGHEST)[0]
        for layer_number in range(LAYERS)
    ]
    stored = []
    for layer_number in range(LAYERS):
        weights = projections[layer_number]
        unit_rows, inverse, normed = normalize(current, film_rows[layer_number], model_width)
        queries = project(normed, weights[0]).astype(jnp.bfloat16)
        key_ext, value_ext = extend_rims(normed, weights, rim_width, model_width)
        pieces = []
        for head_index in range(HEADS):
            head_cols = slice(head_index * head_size, (head_index + 1) * head_size)
            attention = dense_attention(
                queries[:, head_cols], key_ext[:, head_cols], present, head_size
            )
            pieces.append(project(attention.astype(jnp.bfloat16), value_ext[:, head_cols]))
        attended = jnp.concatenate(pieces, axis=1).astype(jnp.bfloat16)
        stored.append((unit_rows, inverse, normed, queries, key_ext, value_ext, attended))
        current = (current.astype(jnp.float32) + project(attended, weights[3])).astype(jnp.bfloat16)
    upstream = cotangent[0]
    weight_list = [None] * LAYERS
    film_list = [None] * LAYERS
    for layer_number in reversed(range(LAYERS)):
        weights = projections[layer_number]
        film_row = film_rows[layer_number]
        unit_rows, inverse, normed, queries, key_ext, value_ext, attended = stored[layer_number]
        grad_out = contract_rows(attended, upstream)
        grad_attended = contract_cols(upstream, weights[3]).astype(jnp.bfloat16)
        query_parts, key_parts, value_parts = ([], [], [])
        for head_index in range(HEADS):
            head_cols = slice(head_index * head_size, (head_index + 1) * head_size)
            attention = dense_attention(
                queries[:, head_cols], key_ext[:, head_cols], present, head_size
            )
            rounded = attention.astype(jnp.bfloat16)
            grad_head = grad_attended[:, head_cols]
            grad_probs = contract_cols(grad_head, value_ext[:, head_cols])
            grad_scores = (
                attention
                * (grad_probs - jnp.sum(attention * grad_probs, axis=1, keepdims=True))
                / math.sqrt(head_size)
            ).astype(jnp.bfloat16)
            query_parts.append(project(grad_scores, key_ext[:, head_cols]))
            key_parts.append(contract_rows(grad_scores, queries[:, head_cols]))
            value_parts.append(contract_rows(rounded, grad_head))
        grad_queries = jnp.concatenate(query_parts, axis=1).astype(jnp.bfloat16)
        rim_terms = jnp.concatenate(key_parts + value_parts, axis=1)
        from_above = from_behind(rim_terms[:rim_width].astype(jnp.bfloat16), "mesh", -1).astype(
            jnp.float32
        )
        from_below = from_behind(
            rim_terms[rim_width + node_count :].astype(jnp.bfloat16), "mesh", 1
        ).astype(jnp.float32)
        owned_rows = rim_terms[rim_width : rim_width + node_count]
        owned_rows = (
            owned_rows
            + jnp.pad(from_below, ((0, node_count - rim_width), (0, 0)))
            + jnp.pad(from_above, ((node_count - rim_width, 0), (0, 0)))
        )
        grad_keys = owned_rows[:, :model_width].astype(jnp.bfloat16)
        grad_values = owned_rows[:, model_width:].astype(jnp.bfloat16)
        weight_list[layer_number] = jnp.stack(
            [
                contract_rows(normed, grad_queries),
                contract_rows(normed, grad_keys),
                contract_rows(normed, grad_values),
                grad_out,
            ]
        )
        grad_normed = (
            contract_cols(grad_queries, weights[0])
            + contract_cols(grad_keys, weights[1])
            + contract_cols(grad_values, weights[2])
        )
        grad_conditioning = jnp.concatenate(
            [jnp.sum(grad_normed * unit_rows, axis=0), jnp.sum(grad_normed, axis=0)]
        )
        film_list[layer_number] = embedding[:, None] * grad_conditioning[None, :]
        grad_unit = grad_normed * (1.0 + film_row[:model_width])
        centred = (
            grad_unit
            - jnp.mean(grad_unit, axis=1, keepdims=True)
            - unit_rows * jnp.mean(grad_unit * unit_rows, axis=1, keepdims=True)
        )
        upstream = (upstream.astype(jnp.float32) + inverse * centred).astype(jnp.bfloat16)
    weight_grads = jnp.stack(weight_list)
    film_grads = jnp.stack(film_list)
    weight_part = lax.psum_scatter(
        weight_grads.astype(jnp.bfloat16), "ens", scatter_dimension=2, tiled=True
    )
    film_part = lax.psum(film_grads.astype(jnp.bfloat16), "ens")
    weight_out, film_out = (
        lax.psum_scatter(weight_part, "mesh", scatter_dimension=3, tiled=True).astype(jnp.float32),
        lax.psum_scatter(film_part, "mesh", scatter_dimension=2, tiled=True).astype(jnp.float32),
    )
    return (upstream[None], weight_out, film_out)


def solution(mesh):
    placed = (
        P("ens", "mesh", None),
        P("ens", "mesh", None),
        P("ens"),
        P("mesh", None),
        P("mesh", None),
        P(),
        P(),
    )
    return jax.shard_map(
        body,
        mesh=mesh,
        in_specs=placed,
        out_specs=(P("ens", "mesh", None), P(None, None, "ens", "mesh"), P(None, None, "mesh")),
        check_vma=False,
    )
```

profile of v0, /device:TPU:0, one launch (start us, length us, event | category | flops | bytes accessed | tf_op | source)
XLA Modules:
  0.0 294.2 jit_solution(6089208120001934512)
XLA Ops:
  9.1 1.2 fusion.37
  10.2 1.1 fusion.115
  11.5 1.6 convolution_convert_fusion.14
  13.1 1.4 convolution_convert_fusion.13
  14.5 2.4 collective-permute-start
  17.0 1.3 collective-permute-start.1
  19.1 56.7 %scatter_custom_fusion = f32[131072]{0:T(1024)S(1)} fusion(s32[8192]{0:T(1024)S(1)} %reshape.328, f32[8192]{0:T(1024)S(1)} %reshape.330, f32[]{:T(128)} %constant.46.clone.1), kind=kCustom, calls=%fused_computation.217 | custom fusion | flops 8192 | bytes 524292
  76.1 1.4 convolution_convert_fusion.15
  83.4 5.1 %collective-permute-start.2 = (bf16[128,1024]{1,0:T(8,128)(2,1)S(1)}, bf16[128,1024]{1,0:T(8,128)(2,1)S(1)}, u32[]{:S(2)}, u32[]{:S(2)}) collective-permute-start(bf16[128,1024]{1,0:T(8,128)(2,1)S(1)} %get-tuple-element.31), channel_id=1, source_target_pairs={{0,1},{1,2},{2,3},{4,5},{5,6},{6,7},{8,9},{9,10},{10,11},{12,13},{... | collective-permute-start | bytes 786440 | tf_op jit(solution)/shard_map/ppermute | solution.py:21
  88.6 1.5 collective-permute-start.3
  90.7 2.5 collective-permute-done.3
  101.5 6.7 %collective-permute-start.4 = (bf16[128,1024]{0,1:T(8,128)(2,1)S(1)}, bf16[128,1024]{0,1:T(8,128)(2,1)S(1)}, u32[]{:S(2)}, u32[]{:S(2)}) collective-permute-start(bf16[128,1024]{0,1:T(8,128)(2,1)S(1)} %get-tuple-element.29), channel_id=1, source_target_pairs={{0,1},{1,2},{2,3},{4,5},{5,6},{6,7},{8,9},{9,10},{10,11},{12,13},{... | collective-permute-start | bytes 786440 | tf_op jit(solution)/shard_map/ppermute | solution.py:33
  108.2 1.3 collective-permute-start.5
  118.9 6.2 %collective-permute-start.6 = (bf16[128,1024]{0,1:T(8,128)(2,1)S(1)}, bf16[128,1024]{0,1:T(8,128)(2,1)S(1)}, u32[]{:S(2)}, u32[]{:S(2)}) collective-permute-start(bf16[128,1024]{0,1:T(8,128)(2,1)S(1)} %get-tuple-element.27), channel_id=1, source_target_pairs={{0,1},{1,2},{2,3},{4,5},{5,6},{6,7},{8,9},{9,10},{10,11},{12,13},{... | collective-permute-start | bytes 786440 | tf_op jit(solution)/shard_map/ppermute | solution.py:33
  125.1 1.5 collective-permute-start.7
  130.0 2.3 pad_maximum_fusion
  132.4 1.4 fusion.56
  133.8 1.4 convolution_add_fusion.1
  135.2 1.6 fusion.36
  137.7 87.3 %reduce-scatter.6.cloned.1.call-done = bf16[2,4,64,512]{3,2,1,0:T(8,128)(2,1)} async-done(((bf16[2,4,512,512]{3,2,1,0:T(8,128)(2,1)}), bf16[2,4,64,512]{3,2,1,0:T(8,128)(2,1)}) %reduce-scatter.6.cloned.1.call-update) | async-done | bytes 524304 | tf_op jit(solution)/shard_map/reduce_scatter | solution.py:196
  224.9 1.6 copy.13
  226.6 1.4 reshape.338
  229.0 18.3 %reduce-scatter.8.cloned.1.call-done = bf16[2,32,256]{2,1,0:T(8,128)(2,1)} async-done(((bf16[2,32,1024]{2,1,0:T(8,128)(2,1)}), bf16[2,32,256]{2,1,0:T(8,128)(2,1)}) %reduce-scatter.8.cloned.1.call-update) | async-done | bytes 32784 | tf_op jit(solution)/shard_map/reduce_scatter | solution.py:202
  247.3 37.8 %psum.8 = bf16[2,32,256]{2,1,0:T(8,128)(2,1)S(1)} all-reduce(bf16[2,32,256]{2,1,0:T(8,128)(2,1)} %reduce-scatter.8.cloned.1.call-done), channel_id=1, replica_groups=mesh['ens'=8,'mesh'=4] {'ens'}, use_global_device_ids=true, to_apply=%region_39.40 | all-reduce | flops 16384 | bytes 65536 | tf_op jit(solution)/shard_map/psum | solution.py:199
  (156 shorter events, 33.9 us)
Async XLA Ops:
  7.2 5.9 %copy-start = (bf16[1,256,512]{2,1,0:T(8,128)(2,1)S(1)}, bf16[1,256,512]{2,1,0:T(8,128)(2,1)}, u32[]{:S(2)}) copy-start(bf16[1,256,512]{2,1,0:T(8,128)(2,1)} %param.7) | copy-start | bytes 786436
  7.2 217.8 %reduce-scatter.6.cloned.1.call-start = ((), (), s32[]{:S(2)}) async-start(), calls=%async_computation.3 | async-start | bytes 4718592 | tf_op jit(solution)/shard_map/reduce_scatter | solution.py:196
  11.4 6.8 %copy-start.2 = (f32[2,32,1024]{2,1,0:T(8,128)S(1)}, f32[2,32,1024]{2,1,0:T(8,128)}, u32[]{:S(2)}) copy-start(f32[2,32,1024]{2,1,0:T(8,128)} %param.13) | copy-start | bytes 786436
  11.4 7.1 %copy-start.4 = (s32[256,32]{0,1:T(8,128)S(1)}, s32[256,32]{0,1:T(8,128)}, u32[]{:S(2)}) copy-start(s32[256,32]{0,1:T(8,128)} %param.10) | copy-start | bytes 98308
  11.4 7.1 %copy-start.7 = (s32[2]{0:T(128)S(1)}, s32[2]{0:T(128)}, u32[]{:S(2)}) copy-start(s32[2]{0:T(128)} %constant.74) | copy-start | bytes 28
  11.4 7.2 %copy-start.6 = (s32[2]{0:T(128)S(1)}, s32[2]{0:T(128)}, u32[]{:S(2)}) copy-start(s32[2]{0:T(128)} %constant.71) | copy-start | bytes 28
  11.5 7.3 %copy-start.5 = (s32[256,32]{0,1:T(8,128)S(1)}, s32[256,32]{0,1:T(8,128)}, u32[]{:S(2)}) copy-start(s32[256,32]{0,1:T(8,128)} %param.11) | copy-start | bytes 98308
  14.5 63.0 %collective-permute-start = (bf16[128,1024]{1,0:T(8,128)(2,1)S(1)}, bf16[128,1024]{1,0:T(8,128)(2,1)S(1)}, u32[]{:S(2)}, u32[]{:S(2)}) collective-permute-start(bf16[128,1024]{1,0:T(8,128)(2,1)S(1)} %get-tuple-element.33), channel_id=1, source_target_pairs={{0,1},{1,2},{2,3},{4,5},{5,6},{6,7},{8,9},{9,10},{10,11},{12,13},{... | collective-permute-start | bytes 786440 | tf_op jit(solution)/shard_map/ppermute | solution.py:21
  17.0 60.6 %collective-permute-start.1 = (bf16[128,1024]{1,0:T(8,128)(2,1)S(1)}, bf16[128,1024]{1,0:T(8,128)(2,1)S(1)}, u32[]{:S(2)}, u32[]{:S(2)}) collective-permute-start(bf16[128,1024]{1,0:T(8,128)(2,1)S(1)} %get-tuple-element.34), channel_id=1, source_target_pairs={{1,0},{2,1},{3,2},{5,4},{6,5},{7,6},{9,8},{10,9},{11,10},{13,12},{... | collective-permute-start | bytes 786440 | tf_op jit(solution)/shard_map/ppermute | solution.py:23
  79.7 2.2 copy-start.1
  82.5 7.5 %copy-start.3 = (bf16[1,256,512]{2,1,0:T(8,128)(2,1)S(1)}, bf16[1,256,512]{2,1,0:T(8,128)(2,1)}, u32[]{:S(2)}) copy-start(bf16[1,256,512]{2,1,0:T(8,128)(2,1)} %param.8) | copy-start | bytes 786436
  83.4 7.3 %collective-permute-start.2 = (bf16[128,1024]{1,0:T(8,128)(2,1)S(1)}, bf16[128,1024]{1,0:T(8,128)(2,1)S(1)}, u32[]{:S(2)}, u32[]{:S(2)}) collective-permute-start(bf16[128,1024]{1,0:T(8,128)(2,1)S(1)} %get-tuple-element.31), channel_id=1, source_target_pairs={{0,1},{1,2},{2,3},{4,5},{5,6},{6,7},{8,9},{9,10},{10,11},{12,13},{... | collective-permute-start | bytes 786440 | tf_op jit(solution)/shard_map/ppermute | solution.py:21
  88.6 4.7 %collective-permute-start.3 = (bf16[128,1024]{1,0:T(8,128)(2,1)S(1)}, bf16[128,1024]{1,0:T(8,128)(2,1)S(1)}, u32[]{:S(2)}, u32[]{:S(2)}) collective-permute-start(bf16[128,1024]{1,0:T(8,128)(2,1)S(1)} %get-tuple-element.32), channel_id=1, source_target_pairs={{1,0},{2,1},{3,2},{5,4},{6,5},{7,6},{9,8},{10,9},{11,10},{13,12},{... | collective-permute-start | bytes 786440 | tf_op jit(solution)/shard_map/ppermute | solution.py:23
  101.5 9.0 %collective-permute-start.4 = (bf16[128,1024]{0,1:T(8,128)(2,1)S(1)}, bf16[128,1024]{0,1:T(8,128)(2,1)S(1)}, u32[]{:S(2)}, u32[]{:S(2)}) collective-permute-start(bf16[128,1024]{0,1:T(8,128)(2,1)S(1)} %get-tuple-element.29), channel_id=1, source_target_pairs={{0,1},{1,2},{2,3},{4,5},{5,6},{6,7},{8,9},{9,10},{10,11},{12,13},{... | collective-permute-start | bytes 786440 | tf_op jit(solution)/shard_map/ppermute | solution.py:33
  108.2 3.4 %collective-permute-start.5 = (bf16[128,1024]{0,1:T(8,128)(2,1)S(1)}, bf16[128,1024]{0,1:T(8,128)(2,1)S(1)}, u32[]{:S(2)}, u32[]{:S(2)}) collective-permute-start(bf16[128,1024]{0,1:T(8,128)(2,1)S(1)} %get-tuple-element.30), channel_id=1, source_target_pairs={{1,0},{2,1},{3,2},{5,4},{6,5},{7,6},{9,8},{10,9},{11,10},{13,12},{... | collective-permute-start | bytes 786440 | tf_op jit(solution)/shard_map/ppermute | solution.py:33
  118.9 8.8 %collective-permute-start.6 = (bf16[128,1024]{0,1:T(8,128)(2,1)S(1)}, bf16[128,1024]{0,1:T(8,128)(2,1)S(1)}, u32[]{:S(2)}, u32[]{:S(2)}) collective-permute-start(bf16[128,1024]{0,1:T(8,128)(2,1)S(1)} %get-tuple-element.27), channel_id=1, source_target_pairs={{0,1},{1,2},{2,3},{4,5},{5,6},{6,7},{8,9},{9,10},{10,11},{12,13},{... | collective-permute-start | bytes 786440 | tf_op jit(solution)/shard_map/ppermute | solution.py:33
  125.1 3.4 %collective-permute-start.7 = (bf16[128,1024]{0,1:T(8,128)(2,1)S(1)}, bf16[128,1024]{0,1:T(8,128)(2,1)S(1)}, u32[]{:S(2)}, u32[]{:S(2)}) collective-permute-start(bf16[128,1024]{0,1:T(8,128)(2,1)S(1)} %get-tuple-element.28), channel_id=1, source_target_pairs={{1,0},{2,1},{3,2},{5,4},{6,5},{7,6},{9,8},{10,9},{11,10},{13,12},{... | collective-permute-start | bytes 786440 | tf_op jit(solution)/shard_map/ppermute | solution.py:33
  132.3 115.0 %reduce-scatter.8.cloned.1.call-start = ((), (), s32[]{:S(2)}) async-start(), calls=%async_computation.4 | async-start | bytes 163840 | tf_op jit(solution)/shard_map/reduce_scatter | solution.py:202
  137.6 148.1 %reduce-scatter.10.cloned.1.call-start = ((), (), s32[]{:S(2)}) async-start(), calls=%async_computation.5 | async-start | bytes 655360
Sparse Core Ops, SparseCore 0:
  132.4 92.4 reduce-scatter.5
  227.9 19.2 reduce-scatter.7
  249.8 21.6 reduce-scatter.9
where the time goes:
time: 295 us; the launch traced here: 294 us
  waiting for transfers between devices  110 us (37%)
  other arithmetic  69.8 us (24%)
  blocking collectives  37.8 us (13%)
  matrix products  29.4 us (10%)
  starting transfers between devices  26.1 us (9%)
  between operations  15.4 us (5%)
  local copies, waits for them, and re-layouts  5.72 us (2%)
    reduce_scatter x1, waiting for transfers between devices, body(): lax.psum_scatter(weight_grads.astype(jnp.bfloat16), 'ens', scatter_dimens...  87.3 us
    unnamed x4, other arithmetic  56.9 us
    psum x1, blocking collectives, body(): film_part = lax.psum(film_grads.astype(jnp.bfloat16), 'ens')  37.8 us
    reduce_scatter x1, waiting for transfers between devices, body(): lax.psum_scatter(film_part, 'mesh', scatter_dimension=2, tiled=True)  18.3 us
    ppermute x4, starting transfers between devices, from_behind(): return lax.ppermute(block, axis, route)  15.7 us
    dot_general x24, matrix products, contract_cols(): lax.dot_general(left_side, right_side, (((1,), (1,)), ((), ())), preferre...  11.8 us
    dot_general x23, matrix products, project(): return jnp.dot(left_side, right_side, preferred_element_type=jnp.float32)  9.49 us
    ppermute x2, starting transfers between devices, padded(): lax.ppermute(tail, axis, [(i, (i + 1) % count) for i in range(ends)])  7.55 us
  transfers between devices with their start and end apart: 11, of which 5 were waited for; matrix products, arithmetic and copies ran while one was open for 24% of the time, Pallas kernels for 0%

commit v1 on v0

--- a/solution.py
+++ b/solution.py
@@ -196,7 +196,7 @@
     weight_part = lax.psum_scatter(
         weight_grads.astype(jnp.bfloat16), "ens", scatter_dimension=2, tiled=True
     )
-    film_part = lax.psum(film_grads.astype(jnp.bfloat16), "ens")
+    film_part = jnp.sum(lax.all_gather(film_grads.astype(jnp.bfloat16), "ens"), axis=0)
     weight_out, film_out = (
         lax.psum_scatter(weight_part, "mesh", scatter_dimension=3, tiled=True).astype(jnp.float32),
         lax.psum_scatter(film_part, "mesh", scatter_dimension=2, tiled=True).astype(jnp.float32),

time: 295 us -> 325 us (1.10)
  waiting for transfers between devices: 110 us -> 171 us
  blocking collectives: 37.8 us -> 0 us
    psum x1 -> x0, blocking collectives: 37.8 us -> none  [body(): film_part = lax.psum(film_grads.astype(jnp.bfloat16), 'ens')]
    all_gather x0 -> x1, waiting for transfers between devices: none -> 35.8 us  [body(): lax.all_gather(film_grads.astype(jnp.bfloat16), 'ens')]
    unnamed x4 -> x5, waiting for transfers between devices: 0.05 us -> 22.7 us
  transfers between devices with their start and end apart: 11 -> 12, of which waited for: 5 -> 7; matrix products, arithmetic and copies ran while one was open for 24% -> 24% of each run, Pallas kernels for 0% -> 0%
where the time goes in v1:
time: 325 us; the launch traced here: 324 us
  waiting for transfers between devices  171 us (53%)
  other arithmetic  72.8 us (22%)
  matrix products  32.4 us (10%)
  starting transfers between devices  26.2 us (8%)
  between operations  15.7 us (5%)
  local copies, waits for them, and re-layouts  5.86 us (2%)
    reduce_scatter x1, waiting for transfers between devices, body(): lax.psum_scatter(weight_grads.astype(jnp.bfloat16), 'ens', scatter_dimens...  88.5 us
    unnamed x4, other arithmetic  56.9 us
    all_gather x1, waiting for transfers between devices, body(): lax.all_gather(film_grads.astype(jnp.bfloat16), 'ens')  35.8 us
    unnamed x5, waiting for transfers between devices  22.7 us
    reduce_scatter x1, waiting for transfers between devices, body(): lax.psum_scatter(film_part, 'mesh', scatter_dimension=2, tiled=True)  18.2 us
    ppermute x4, starting transfers between devices, from_behind(): return lax.ppermute(block, axis, route)  15.5 us
    dot_general x23, matrix products, project(): return jnp.dot(left_side, right_side, preferred_element_type=jnp.float32)  11.4 us
    dot_general x24, matrix products, contract_cols(): lax.dot_general(left_side, right_side, (((1,), (1,)), ((), ())), preferre...  10.9 us
  transfers between devices with their start and end apart: 12, of which 7 were waited for; matrix products, arithmetic and copies ran while one was open for 24% of the time, Pallas kernels for 0%

profile of v1, /device:TPU:0, one launch (start us, length us, event | category | flops | bytes accessed | tf_op | source)
XLA Modules:
  0.0 324.4 jit_solution(3812214077521883231)
XLA Ops:
  11.5 1.6 convolution_convert_fusion.14
  13.1 1.4 convolution_convert_fusion.13
  14.6 2.4 collective-permute-start
  19.2 1.4 convolution_convert_fusion.9
  20.6 56.7 %scatter_custom_fusion = f32[131072]{0:T(1024)S(1)} fusion(s32[8192]{0:T(1024)S(1)} %reshape.389, f32[8192]{0:T(1024)S(1)} %reshape.391, f32[]{:T(128)} %constant.47.clone.1), kind=kCustom, calls=%fused_computation.217 | custom fusion | flops 8192 | bytes 524292
  77.6 1.4 convolution_convert_fusion.15
  85.0 5.2 %collective-permute-start.2 = (bf16[128,1024]{1,0:T(8,128)(2,1)S(1)}, bf16[128,1024]{1,0:T(8,128)(2,1)S(1)}, u32[]{:S(2)}, u32[]{:S(2)}) collective-permute-start(bf16[128,1024]{1,0:T(8,128)(2,1)S(1)} %get-tuple-element.31), channel_id=1, source_target_pairs={{0,1},{1,2},{2,3},{4,5},{5,6},{6,7},{8,9},{9,10},{10,11},{12,13},{... | collective-permute-start | bytes 786440 | tf_op jit(solution)/shard_map/ppermute | solution.py:21
  90.1 1.5 collective-permute-start.3
  92.0 2.8 collective-permute-done.3
  104.5 6.7 %collective-permute-start.4 = (bf16[128,1024]{0,1:T(8,128)(2,1)S(1)}, bf16[128,1024]{0,1:T(8,128)(2,1)S(1)}, u32[]{:S(2)}, u32[]{:S(2)}) collective-permute-start(bf16[128,1024]{0,1:T(8,128)(2,1)S(1)} %get-tuple-element.29), channel_id=1, source_target_pairs={{0,1},{1,2},{2,3},{4,5},{5,6},{6,7},{8,9},{9,10},{10,11},{12,13},{... | collective-permute-start | bytes 786440 | tf_op jit(solution)/shard_map/ppermute | solution.py:33
  113.2 1.5 collective-permute-done.5
  121.4 6.2 %collective-permute-start.6 = (bf16[128,1024]{0,1:T(8,128)(2,1)S(1)}, bf16[128,1024]{0,1:T(8,128)(2,1)S(1)}, u32[]{:S(2)}, u32[]{:S(2)}) collective-permute-start(bf16[128,1024]{0,1:T(8,128)(2,1)S(1)} %get-tuple-element.27), channel_id=1, source_target_pairs={{0,1},{1,2},{2,3},{4,5},{5,6},{6,7},{8,9},{9,10},{10,11},{12,13},{... | collective-permute-start | bytes 786440 | tf_op jit(solution)/shard_map/ppermute | solution.py:33
  129.3 1.7 collective-permute-done.7
  131.5 1.8 fusion.36
  136.0 1.4 fusion.7
  140.6 2.3 pad_maximum_fusion
  142.9 35.8 %all-gather.2.cloned.1.call-done = bf16[8,2,32,1024]{3,2,1,0:T(8,128)(2,1)} async-done(((bf16[1,2,32,1024]{3,2,1,0:T(8,128)(2,1)}), bf16[8,2,32,1024]{3,2,1,0:T(8,128)(2,1)}) %all-gather.2.cloned.1.call-update) | async-done | bytes 1048592 | tf_op jit(solution)/shard_map/all_gather | solution.py:199
  178.8 2.1 reduce_sum.324
  180.9 88.5 %reduce-scatter.6.cloned.1.call-done = bf16[2,4,64,512]{3,2,1,0:T(8,128)(2,1)} async-done(((bf16[2,4,512,512]{3,2,1,0:T(8,128)(2,1)}), bf16[2,4,64,512]{3,2,1,0:T(8,128)(2,1)}) %reduce-scatter.6.cloned.1.call-update) | async-done | bytes 524304 | tf_op jit(solution)/shard_map/reduce_scatter | solution.py:196
  269.5 1.6 copy.13
  271.1 1.4 reshape.399
  273.5 18.2 %reduce-scatter.8.cloned.1.call-done = bf16[2,32,256]{2,1,0:T(8,128)(2,1)} async-done(((bf16[2,32,1024]{2,1,0:T(8,128)(2,1)}), bf16[2,32,256]{2,1,0:T(8,128)(2,1)}) %reduce-scatter.8.cloned.1.call-update) | async-done | bytes 32784 | tf_op jit(solution)/shard_map/reduce_scatter | solution.py:202
  291.8 1.4 convert_element_type.216
  293.2 22.6 %reduce-scatter.10.cloned.1.call-done = bf16[128,512]{1,0:T(8,128)(2,1)} async-done(((bf16[512,512]{1,0:T(8,128)(2,1)}), bf16[128,512]{1,0:T(8,128)(2,1)}) %reduce-scatter.10.cloned.1.call-update) | async-done | bytes 131088
  (207 shorter events, 40.9 us)
Async XLA Ops:
  7.2 171.6 %all-gather.2.cloned.1.call-start = ((), (), s32[]{:S(2)}) async-start(), calls=%async_computation.4 | async-start | bytes 1179648 | tf_op jit(solution)/shard_map/all_gather | solution.py:199
  11.4 66.2 %copy-start.26 = (f32[512]{0:T(512)}, f32[512]{0:T(512)S(1)}, u32[]{:S(2)}) copy-start(f32[512]{0:T(512)S(1)} %get-tuple-element.48) | copy-start | bytes 6148
  11.4 7.2 %copy-start.31 = (s32[2]{0:T(128)S(1)}, s32[2]{0:T(128)}, u32[]{:S(2)}) copy-start(s32[2]{0:T(128)} %constant.75) | copy-start | bytes 28
  11.5 7.2 %copy-start.30 = (s32[2]{0:T(128)S(1)}, s32[2]{0:T(128)}, u32[]{:S(2)}) copy-start(s32[2]{0:T(128)} %constant.72) | copy-start | bytes 28
  11.5 7.3 %copy-start.25 = (s32[256,32]{0,1:T(8,128)S(1)}, s32[256,32]{0,1:T(8,128)}, u32[]{:S(2)}) copy-start(s32[256,32]{0,1:T(8,128)} %param.11) | copy-start | bytes 98308
  14.6 64.4 %collective-permute-start = (bf16[128,1024]{1,0:T(8,128)(2,1)S(1)}, bf16[128,1024]{1,0:T(8,128)(2,1)S(1)}, u32[]{:S(2)}, u32[]{:S(2)}) collective-permute-start(bf16[128,1024]{1,0:T(8,128)(2,1)S(1)} %get-tuple-element.33), channel_id=1, source_target_pairs={{0,1},{1,2},{2,3},{4,5},{5,6},{6,7},{8,9},{9,10},{10,11},{12,13},{... | collective-permute-start | bytes 786440 | tf_op jit(solution)/shard_map/ppermute | solution.py:21
  17.0 62.0 %collective-permute-start.1 = (bf16[128,1024]{1,0:T(8,128)(2,1)S(1)}, bf16[128,1024]{1,0:T(8,128)(2,1)S(1)}, u32[]{:S(2)}, u32[]{:S(2)}) collective-permute-start(bf16[128,1024]{1,0:T(8,128)(2,1)S(1)} %get-tuple-element.34), channel_id=1, source_target_pairs={{1,0},{2,1},{3,2},{5,4},{6,5},{7,6},{9,8},{10,9},{11,10},{13,12},{... | collective-permute-start | bytes 786440 | tf_op jit(solution)/shard_map/ppermute | solution.py:23
  85.0 7.0 %collective-permute-start.2 = (bf16[128,1024]{1,0:T(8,128)(2,1)S(1)}, bf16[128,1024]{1,0:T(8,128)(2,1)S(1)}, u32[]{:S(2)}, u32[]{:S(2)}) collective-permute-start(bf16[128,1024]{1,0:T(8,128)(2,1)S(1)} %get-tuple-element.31), channel_id=1, source_target_pairs={{0,1},{1,2},{2,3},{4,5},{5,6},{6,7},{8,9},{9,10},{10,11},{12,13},{... | collective-permute-start | bytes 786440 | tf_op jit(solution)/shard_map/ppermute | solution.py:21
  90.1 4.7 %collective-permute-start.3 = (bf16[128,1024]{1,0:T(8,128)(2,1)S(1)}, bf16[128,1024]{1,0:T(8,128)(2,1)S(1)}, u32[]{:S(2)}, u32[]{:S(2)}) collective-permute-start(bf16[128,1024]{1,0:T(8,128)(2,1)S(1)} %get-tuple-element.32), channel_id=1, source_target_pairs={{1,0},{2,1},{3,2},{5,4},{6,5},{7,6},{9,8},{10,9},{11,10},{13,12},{... | collective-permute-start | bytes 786440 | tf_op jit(solution)/shard_map/ppermute | solution.py:23
  102.6 10.2 %copy-start.6 = (bf16[256,128]{0,1:T(8,128)(2,1)}, bf16[256,128]{0,1:T(8,128)(2,1)S(1)}, u32[]{:S(2)}) copy-start(bf16[256,128]{0,1:T(8,128)(2,1)S(1)} %convolution_convert_fusion.25) | copy-start | bytes 196612
  104.5 8.6 %collective-permute-start.4 = (bf16[128,1024]{0,1:T(8,128)(2,1)S(1)}, bf16[128,1024]{0,1:T(8,128)(2,1)S(1)}, u32[]{:S(2)}, u32[]{:S(2)}) collective-permute-start(bf16[128,1024]{0,1:T(8,128)(2,1)S(1)} %get-tuple-element.29), channel_id=1, source_target_pairs={{0,1},{1,2},{2,3},{4,5},{5,6},{6,7},{8,9},{9,10},{10,11},{12,13},{... | collective-permute-start | bytes 786440 | tf_op jit(solution)/shard_map/ppermute | solution.py:33
  111.2 3.4 %collective-permute-start.5 = (bf16[128,1024]{0,1:T(8,128)(2,1)S(1)}, bf16[128,1024]{0,1:T(8,128)(2,1)S(1)}, u32[]{:S(2)}, u32[]{:S(2)}) collective-permute-start(bf16[128,1024]{0,1:T(8,128)(2,1)S(1)} %get-tuple-element.30), channel_id=1, source_target_pairs={{1,0},{2,1},{3,2},{5,4},{6,5},{7,6},{9,8},{10,9},{11,10},{13,12},{... | collective-permute-start | bytes 786440 | tf_op jit(solution)/shard_map/ppermute | solution.py:33
  118.1 10.8 %copy-start.8 = (bf16[256,128]{0,1:T(8,128)(2,1)}, bf16[256,128]{0,1:T(8,128)(2,1)S(1)}, u32[]{:S(2)}) copy-start(bf16[256,128]{0,1:T(8,128)(2,1)S(1)} %convolution_convert_fusion.23) | copy-start | bytes 196612
  118.7 10.1 %copy-start.10 = (bf16[256,128]{0,1:T(8,128)(2,1)}, bf16[256,128]{0,1:T(8,128)(2,1)S(1)}, u32[]{:S(2)}) copy-start(bf16[256,128]{0,1:T(8,128)(2,1)S(1)} %convolution_convert_fusion.20) | copy-start | bytes 196612
  119.1 9.7 %copy-start.12 = (bf16[256,128]{0,1:T(8,128)(2,1)}, bf16[256,128]{0,1:T(8,128)(2,1)S(1)}, u32[]{:S(2)}) copy-start(bf16[256,128]{0,1:T(8,128)(2,1)S(1)} %convolution_convert_fusion.21) | copy-start | bytes 196612
  119.6 9.4 %copy-start.14 = (bf16[256,128]{0,1:T(8,128)(2,1)}, bf16[256,128]{0,1:T(8,128)(2,1)S(1)}, u32[]{:S(2)}) copy-start(bf16[256,128]{0,1:T(8,128)(2,1)S(1)} %convolution_convert_fusion.22) | copy-start | bytes 196612
  121.4 7.9 %collective-permute-start.6 = (bf16[128,1024]{0,1:T(8,128)(2,1)S(1)}, bf16[128,1024]{0,1:T(8,128)(2,1)S(1)}, u32[]{:S(2)}, u32[]{:S(2)}) collective-permute-start(bf16[128,1024]{0,1:T(8,128)(2,1)S(1)} %get-tuple-element.27), channel_id=1, source_target_pairs={{0,1},{1,2},{2,3},{4,5},{5,6},{6,7},{8,9},{9,10},{10,11},{12,13},{... | collective-permute-start | bytes 786440 | tf_op jit(solution)/shard_map/ppermute | solution.py:33
  127.6 3.4 %collective-permute-start.7 = (bf16[128,1024]{0,1:T(8,128)(2,1)S(1)}, bf16[128,1024]{0,1:T(8,128)(2,1)S(1)}, u32[]{:S(2)}, u32[]{:S(2)}) collective-permute-start(bf16[128,1024]{0,1:T(8,128)(2,1)S(1)} %get-tuple-element.28), channel_id=1, source_target_pairs={{1,0},{2,1},{3,2},{5,4},{6,5},{7,6},{9,8},{10,9},{11,10},{13,12},{... | collective-permute-start | bytes 786440 | tf_op jit(solution)/shard_map/ppermute | solution.py:33
  134.1 135.3 %reduce-scatter.6.cloned.1.call-start = ((), (), s32[]{:S(2)}) async-start(), calls=%async_computation.3 | async-start | bytes 4718592 | tf_op jit(solution)/shard_map/reduce_scatter | solution.py:196
  142.9 148.9 %reduce-scatter.8.cloned.1.call-start = ((), (), s32[]{:S(2)}) async-start(), calls=%async_computation.5 | async-start | bytes 163840 | tf_op jit(solution)/shard_map/reduce_scatter | solution.py:202
  180.9 91.7 %copy-start.29 = (f32[256]{0:T(256)S(1)}, f32[256]{0:T(256)}, u32[]{:S(2)}) copy-start(f32[256]{0:T(256)} %get-tuple-element.6) | copy-start | bytes 3076
  180.9 91.7 %copy-start.28 = (f32[256]{0:T(256)S(1)}, f32[256]{0:T(256)}, u32[]{:S(2)}) copy-start(f32[256]{0:T(256)} %get-tuple-element.7) | copy-start | bytes 3076
  180.9 91.7 %copy-start.1 = (f32[256,512]{1,0:T(8,128)S(1)}, f32[256,512]{1,0:T(8,128)}, u32[]{:S(2)}) copy-start(f32[256,512]{1,0:T(8,128)} %get-tuple-element.79) | copy-start | bytes 1572868
  180.9 134.9 %reduce-scatter.10.cloned.1.call-start = ((), (), s32[]{:S(2)}) async-start(), calls=%async_computation.6 | async-start | bytes 655360
  (20 other events, 64.5 us)
Sparse Core Ops, SparseCore 0:
  134.3 44.4 all-gather.1
  182.4 87.0 reduce-scatter.5
  272.5 19.2 reduce-scatter.7
  294.1 21.6 reduce-scatter.9
